TPU v7x, 32 devices: a whole 2x2x4 slice. The times are simulated.
32 devices in a mesh: kz: 4 (over x, core), en: 8 (over z, y).
Axes of the slice: x: 2, y: 2, z: 4, core: 2. Of those that a mesh axis runs over, the one named last changes fastest.
Arguments:
- green_blocks: float32 [4, 16, 2, 256, 256], P('kz', 'en'), may hold values from -6 to 6
- couplings: float32 [4, 8, 2, 256, 256], P('kz', 'en'), may hold values from -0.375 to 0.375
- owners: int32 [2], replicated, may hold values from 0 to 31
- momentum_shift: int32 [2], replicated, may hold values from -3 to 3
- energy_shift: int32 [2], replicated, may hold values from 1 to 7
Outputs:
- self_energy: float32 [4, 16, 2, 256, 256], P('kz', 'en')
Inputs may be any that keep to these rules, and one draw needn't show every extreme that they name: `owners`: flat device index of each mode's coupling block.
All inputs are finite; a program needn't handle non-finite values.
Results may differ from a plain program's by a relative error of at most 0.0001.
Values sent between devices are 32-bit elements; how exact they have to be, the bound alone decides.
No kernel may reach another device: no remote copies, remote signals or barrier semaphores. Data moves between devices by JAX's collectives and lax.ppermute only.
A program may use at most 64 MiB of HBM per device.

v0:
```python
import jax
import jax.numpy as jnp
from jax import lax
from jax.sharding import PartitionSpec as P


def spread(array, axis, root):
    mine = lax.axis_index(axis) == root
    return lax.psum(jnp.where(mine, array, jnp.zeros_like(array)), axis)


def passed_along(block, axis, distance):
    devices = range(lax.axis_size(axis))
    route = [(i - distance, i) for i in devices if i - distance in devices]
    return lax.ppermute(block, axis, route)


def shifted(array, axis, by):
    devices = lax.axis_size(axis)
    return lax.ppermute(array, axis, [(i, (i + by) % devices) for i in range(devices)])


def matmul_left(left, right):
    return jnp.einsum("ij,...jk->...ik", left, right, precision=lax.Precision.HIGHEST)


def matmul_right(left, right):
    return jnp.einsum("...ij,kj->...ik", left, right, precision=lax.Precision.HIGHEST)


def sandwich(coupling, blocks):
    couple_real = coupling[0]
    couple_imag = coupling[1]
    green_real = blocks[..., 0, :, :]
    green_imag = blocks[..., 1, :, :]
    left_real = matmul_left(couple_real, green_real) - matmul_left(couple_imag, green_imag)
    left_imag = matmul_left(couple_real, green_imag) + matmul_left(couple_imag, green_real)
    out_real = matmul_right(left_real, couple_real) + matmul_right(left_imag, couple_imag)
    out_imag = matmul_right(left_imag, couple_real) - matmul_right(left_real, couple_imag)
    return jnp.stack([out_real, out_imag], axis=-3)


def pick_energies(own_blocks, lower_blocks, shift_value):
    local_count = own_blocks.shape[1]
    joined = jnp.concatenate([lower_blocks, own_blocks], axis=1)
    start = local_count - shift_value
    return lax.dynamic_slice_in_dim(joined, start, local_count, 1)


def bit_set(shift_value, bit_index):
    return shift_value // (1 << bit_index) % 2 == 1


def shards(green_blocks, couplings, owners, momentum_shift, energy_shift):
    coupling_list = []
    for mode_index in range(2):
        coupling_list.append(spread(couplings[0, 0], ("kz", "en"), owners[mode_index]))
    momentum_count = lax.axis_size("kz")
    bit_count = (momentum_count - 1).bit_length()
    local_count = green_blocks.shape[1]
    momentum_first = jnp.mod(momentum_shift[0], momentum_count)
    momentum_second = jnp.mod(momentum_shift[1], momentum_count)
    lower_blocks = passed_along(green_blocks, "en", 1)
    first = pick_energies(green_blocks, lower_blocks, energy_shift[0] % local_count)
    second = pick_energies(green_blocks, lower_blocks, energy_shift[1] % local_count)
    steps_first = energy_shift[0] // local_count
    steps_second = energy_shift[1] // local_count
    for bit_index in range(2):
        moved = passed_along((first, second), "en", 1 << bit_index)
        first = jnp.where(bit_set(steps_first, bit_index), moved[0], first)
        second = jnp.where(bit_set(steps_second, bit_index), moved[1], second)
    for bit_index in range(bit_count):
        moved = shifted((first, second), "kz", 1 << bit_index)
        first = jnp.where(bit_set(momentum_first, bit_index), moved[0], first)
        second = jnp.where(bit_set(momentum_second, bit_index), moved[1], second)
    first_term = sandwich(coupling_list[0], first)
    second_term = sandwich(coupling_list[1], second)
    result = first_term
    result = result + second_term
    return result


def solution(mesh):
    in_specs = (P("kz", "en", None, None, None), P("kz", "en", None, None, None), P(), P(), P())
    out_specs = P("kz", "en", None, None, None)
    return jax.shard_map(shards, mesh=mesh, in_specs=in_specs, out_specs=out_specs, check_vma=False)
```

profile of v0, /device:TPU:0, one launch (start us, length us, event | category | flops | bytes accessed | tf_op | source)
XLA Modules:
  0.0 311.8 jit_solution(17990503644076765318)
XLA Ops:
  6.5 1.6 copy.6
  8.1 5.9 %collective-permute-start = (f32[1,2,2,256,256]{3,4,1,2,0:T(8,128)S(1)}, f32[1,2,2,256,256]{3,4,1,2,0:T(8,128)}, u32[]{:S(2)}, u32[]{:S(2)}) collective-permute-start(f32[1,2,2,256,256]{3,4,1,2,0:T(8,128)S(1)} %copy.6), channel_id=1, source_target_pairs={{0,1},{1,2},{2,3},{3,4},{4,5},{5,6},{6,7},{8,9},{9,10},{10,11},{11... | collective-permute-start | bytes 3145736 | tf_op jit(solution)/shard_map/ppermute | solution.py:15
  18.5 17.0 %collective-permute-done = f32[1,2,2,256,256]{3,4,1,2,0:T(8,128)} collective-permute-done((f32[1,2,2,256,256]{3,4,1,2,0:T(8,128)S(1)}, f32[1,2,2,256,256]{3,4,1,2,0:T(8,128)}, u32[]{:S(2)}, u32[]{:S(2)}) %collective-permute-start) | collective-permute-done | bytes 1048608 | tf_op jit(solution)/shard_map/ppermute | solution.py:15
  35.7 4.6 %collective-permute-start.5 = (f32[1,2,2,256,256]{3,4,1,2,0:T(8,128)S(1)}, f32[1,2,2,256,256]{3,4,1,2,0:T(8,128)S(1)}, u32[]{:S(2)}, u32[]{:S(2)}) collective-permute-start(f32[1,2,2,256,256]{3,4,1,2,0:T(8,128)S(1)} %get-tuple-element.7), channel_id=1, source_target_pairs={{0,1},{1,2},{2,3},{3,4},{4,5},{5,6},{6,7},{8,9},{9,10},{10,11},{11... | collective-permute-start | bytes 3145736 | tf_op jit(solution)/shard_map/ppermute | solution.py:15
  40.3 5.2 %collective-permute-start.1 = (f32[1,2,2,256,256]{3,4,1,2,0:T(8,128)S(1)}, f32[1,2,2,256,256]{3,4,1,2,0:T(8,128)}, u32[]{:S(2)}, u32[]{:S(2)}) collective-permute-start(f32[1,2,2,256,256]{3,4,1,2,0:T(8,128)S(1)} %get-tuple-element.8), channel_id=1, source_target_pairs={{0,1},{1,2},{2,3},{3,4},{4,5},{5,6},{6,7},{8,9},{9,10},{10,11},{11... | collective-permute-start | bytes 3145736 | tf_op jit(solution)/shard_map/ppermute | solution.py:15
  46.2 17.5 %collective-permute-done.5 = f32[1,2,2,256,256]{3,4,1,2,0:T(8,128)S(1)} collective-permute-done((f32[1,2,2,256,256]{3,4,1,2,0:T(8,128)S(1)}, f32[1,2,2,256,256]{3,4,1,2,0:T(8,128)S(1)}, u32[]{:S(2)}, u32[]{:S(2)}) %collective-permute-start.5) | collective-permute-done | bytes 1048608 | tf_op jit(solution)/shard_map/ppermute | solution.py:15
  63.7 1.1 broadcast_select_fusion
  64.8 7.2 %collective-permute-start.6 = (f32[1,2,2,256,256]{3,4,1,2,0:T(8,128)}, f32[1,2,2,256,256]{3,4,1,2,0:T(8,128)}, u32[]{:S(2)}, u32[]{:S(2)}) collective-permute-start(f32[1,2,2,256,256]{3,4,1,2,0:T(8,128)} %broadcast_select_fusion), channel_id=1, source_target_pairs={{0,2},{1,3},{2,4},{3,5},{4,6},{5,7},{8,10},{9,11},{10,12},{11,13},... | collective-permute-start | bytes 3145736 | tf_op jit(solution)/shard_map/ppermute | solution.py:15
  72.7 11.5 %collective-permute-done.1 = f32[1,2,2,256,256]{3,4,1,2,0:T(8,128)} collective-permute-done((f32[1,2,2,256,256]{3,4,1,2,0:T(8,128)S(1)}, f32[1,2,2,256,256]{3,4,1,2,0:T(8,128)}, u32[]{:S(2)}, u32[]{:S(2)}) %collective-permute-start.1) | collective-permute-done | bytes 1048608 | tf_op jit(solution)/shard_map/ppermute | solution.py:15
  84.2 1.4 broadcast_select_fusion.4
  85.6 9.3 %collective-permute-start.2 = (f32[1,2,2,256,256]{3,4,1,2,0:T(8,128)S(1)}, f32[1,2,2,256,256]{3,4,1,2,0:T(8,128)}, u32[]{:S(2)}, u32[]{:S(2)}) collective-permute-start(f32[1,2,2,256,256]{3,4,1,2,0:T(8,128)S(1)} %broadcast_select_fusion.4), channel_id=1, source_target_pairs={{0,2},{1,3},{2,4},{3,5},{4,6},{5,7},{8,10},{9,11},{10,12},{11,13},... | collective-permute-start | bytes 3145736 | tf_op jit(solution)/shard_map/ppermute | solution.py:15
  94.9 1.4 broadcast_select_fusion.1
  96.4 16.2 %collective-permute-done.2 = f32[1,2,2,256,256]{3,4,1,2,0:T(8,128)} collective-permute-done((f32[1,2,2,256,256]{3,4,1,2,0:T(8,128)S(1)}, f32[1,2,2,256,256]{3,4,1,2,0:T(8,128)}, u32[]{:S(2)}, u32[]{:S(2)}) %collective-permute-start.2) | collective-permute-done | bytes 1048608 | tf_op jit(solution)/shard_map/ppermute | solution.py:15
  112.6 1.4 broadcast_select_fusion.5
  116.8 1.4 broadcast_select_fusion.2
  118.2 1.6 collective-permute-start.8
  123.6 11.6 %collective-permute-done.3 = f32[1,2,2,256,256]{3,4,1,2,0:T(8,128)} collective-permute-done((f32[1,2,2,256,256]{3,4,1,2,0:T(8,128)S(1)}, f32[1,2,2,256,256]{3,4,1,2,0:T(8,128)}, u32[]{:S(2)}, u32[]{:S(2)}) %collective-permute-start.3) | collective-permute-done | bytes 1048608 | tf_op jit(solution)/shard_map/ppermute | solution.py:20
  135.3 1.6 collective-permute-start.4
  136.9 1.1 select_bitcast_fusion
  138.0 6.4 %collective-permute-done.8 = f32[1,2,2,256,256]{3,4,1,2,0:T(8,128)} collective-permute-done((f32[1,2,2,256,256]{3,4,1,2,0:T(8,128)S(1)}, f32[1,2,2,256,256]{3,4,1,2,0:T(8,128)}, u32[]{:S(2)}, u32[]{:S(2)}) %collective-permute-start.8) | collective-permute-done | bytes 1048608 | tf_op jit(solution)/shard_map/ppermute | solution.py:20
  144.4 1.4 broadcast_select_fusion.3
  145.8 142.2 %all-reduce.3.cloned.1.call-done = (f32[2,256,256]{2,1,0:T(8,128)}, f32[2,256,256]{2,1,0:T(8,128)}) async-done(((f32[2,256,256]{2,1,0:T(8,128)}, f32[2,256,256]{2,1,0:T(8,128)}), (f32[2,256,256]{2,1,0:T(8,128)}, f32[2,256,256]{2,1,0:T(8,128)})) %all-reduce.3.cloned.1.call-update) | async-done | bytes 1048592 | tf_op jit(solution)/shard_map/psum | solution.py:9
  288.0 1.6 fusion.13
  290.3 1.4 broadcast_select_fusion.7
  295.3 1.0 fusion.16
  296.3 1.0 fusion.1
  297.3 1.0 fusion
  299.0 1.0 fusion.15
  300.6 1.0 fusion.14
  301.7 1.0 fusion.5
  302.7 1.0 fusion.4
  303.9 1.0 copy.16
  (33 shorter events, 8.0 us)
Async XLA Ops:
  6.5 7.5 %copy-start.3 = (s32[2]{0:T(128)S(1)}, s32[2]{0:T(128)}, u32[]{:S(2)}) copy-start(s32[2]{0:T(128)} %param.9) | copy-start | bytes 28
  6.5 281.5 %all-reduce.3.cloned.1.call-start = ((), (), s32[]{:S(2)}) async-start(), calls=%async_computation | async-start | bytes 2097152 | tf_op jit(solution)/shard_map/psum | solution.py:9
  8.1 27.3 %collective-permute-start = (f32[1,2,2,256,256]{3,4,1,2,0:T(8,128)S(1)}, f32[1,2,2,256,256]{3,4,1,2,0:T(8,128)}, u32[]{:S(2)}, u32[]{:S(2)}) collective-permute-start(f32[1,2,2,256,256]{3,4,1,2,0:T(8,128)S(1)} %copy.6), channel_id=1, source_target_pairs={{0,1},{1,2},{2,3},{3,4},{4,5},{5,6},{6,7},{8,9},{9,10},{10,11},{11... | collective-permute-start | bytes 3145736 | tf_op jit(solution)/shard_map/ppermute | solution.py:15
  35.7 28.0 %collective-permute-start.5 = (f32[1,2,2,256,256]{3,4,1,2,0:T(8,128)S(1)}, f32[1,2,2,256,256]{3,4,1,2,0:T(8,128)S(1)}, u32[]{:S(2)}, u32[]{:S(2)}) collective-permute-start(f32[1,2,2,256,256]{3,4,1,2,0:T(8,128)S(1)} %get-tuple-element.7), channel_id=1, source_target_pairs={{0,1},{1,2},{2,3},{3,4},{4,5},{5,6},{6,7},{8,9},{9,10},{10,11},{11... | collective-permute-start | bytes 3145736 | tf_op jit(solution)/shard_map/ppermute | solution.py:15
  40.3 43.9 %collective-permute-start.1 = (f32[1,2,2,256,256]{3,4,1,2,0:T(8,128)S(1)}, f32[1,2,2,256,256]{3,4,1,2,0:T(8,128)}, u32[]{:S(2)}, u32[]{:S(2)}) collective-permute-start(f32[1,2,2,256,256]{3,4,1,2,0:T(8,128)S(1)} %get-tuple-element.8), channel_id=1, source_target_pairs={{0,1},{1,2},{2,3},{3,4},{4,5},{5,6},{6,7},{8,9},{9,10},{10,11},{11... | collective-permute-start | bytes 3145736 | tf_op jit(solution)/shard_map/ppermute | solution.py:15
  64.8 30.1 %collective-permute-start.6 = (f32[1,2,2,256,256]{3,4,1,2,0:T(8,128)}, f32[1,2,2,256,256]{3,4,1,2,0:T(8,128)}, u32[]{:S(2)}, u32[]{:S(2)}) collective-permute-start(f32[1,2,2,256,256]{3,4,1,2,0:T(8,128)} %broadcast_select_fusion), channel_id=1, source_target_pairs={{0,2},{1,3},{2,4},{3,5},{4,6},{5,7},{8,10},{9,11},{10,12},{11,13},... | collective-permute-start | bytes 3145736 | tf_op jit(solution)/shard_map/ppermute | solution.py:15
  85.6 27.0 %collective-permute-start.2 = (f32[1,2,2,256,256]{3,4,1,2,0:T(8,128)S(1)}, f32[1,2,2,256,256]{3,4,1,2,0:T(8,128)}, u32[]{:S(2)}, u32[]{:S(2)}) collective-permute-start(f32[1,2,2,256,256]{3,4,1,2,0:T(8,128)S(1)} %broadcast_select_fusion.4), channel_id=1, source_target_pairs={{0,2},{1,3},{2,4},{3,5},{4,6},{5,7},{8,10},{9,11},{10,12},{11,13},... | collective-permute-start | bytes 3145736 | tf_op jit(solution)/shard_map/ppermute | solution.py:15
  96.3 20.6 %collective-permute-start.7 = (f32[1,2,2,256,256]{3,4,1,2,0:T(8,128)S(1)}, f32[1,2,2,256,256]{3,4,1,2,0:T(8,128)}, u32[]{:S(2)}, u32[]{:S(2)}) collective-permute-start(f32[1,2,2,256,256]{3,4,1,2,0:T(8,128)S(1)} %broadcast_select_fusion.1), channel_id=1, source_target_pairs={{0,8},{8,16},{16,24},{24,0},{1,9},{9,17},{17,25},{25,1},{2,10},{10... | collective-permute-start | bytes 3145736 | tf_op jit(solution)/shard_map/ppermute | solution.py:20
  96.4 17.9 %copy-start.4 = (s32[2]{0:T(128)S(1)}, s32[2]{0:T(128)}, u32[]{:S(2)}) copy-start(s32[2]{0:T(128)} %param.8) | copy-start | bytes 28
  114.0 21.2 %collective-permute-start.3 = (f32[1,2,2,256,256]{3,4,1,2,0:T(8,128)S(1)}, f32[1,2,2,256,256]{3,4,1,2,0:T(8,128)}, u32[]{:S(2)}, u32[]{:S(2)}) collective-permute-start(f32[1,2,2,256,256]{3,4,1,2,0:T(8,128)S(1)} %broadcast_select_fusion.5), channel_id=1, source_target_pairs={{0,8},{8,16},{16,24},{24,0},{1,9},{9,17},{17,25},{25,1},{2,10},{10... | collective-permute-start | bytes 3145736 | tf_op jit(solution)/shard_map/ppermute | solution.py:20
  116.8 4.9 %copy-start.5 = (s32[2]{0:T(128)S(1)}, s32[2]{0:T(128)}, u32[]{:S(2)}) copy-start(s32[2]{0:T(128)} %param.7) | copy-start | bytes 28
  118.2 26.2 %collective-permute-start.8 = (f32[1,2,2,256,256]{3,4,1,2,0:T(8,128)S(1)}, f32[1,2,2,256,256]{3,4,1,2,0:T(8,128)}, u32[]{:S(2)}, u32[]{:S(2)}) collective-permute-start(f32[1,2,2,256,256]{3,4,1,2,0:T(8,128)S(1)} %broadcast_select_fusion.2), channel_id=1, source_target_pairs={{0,16},{8,24},{16,0},{24,8},{1,17},{9,25},{17,1},{25,9},{2,18},{10... | collective-permute-start | bytes 3145736 | tf_op jit(solution)/shard_map/ppermute | solution.py:20
  123.5 13.3 %copy-start.2 = (f32[1,1,2,256,256]{4,3,2,1,0:T(8,128)S(1)}, f32[1,1,2,256,256]{4,3,2,1,0:T(8,128)}, u32[]{:S(2)}) copy-start(f32[1,1,2,256,256]{4,3,2,1,0:T(8,128)} %param.6) | copy-start | bytes 1572868
  135.3 155.0 %collective-permute-start.4 = (f32[1,2,2,256,256]{3,4,1,2,0:T(8,128)S(1)}, f32[1,2,2,256,256]{3,4,1,2,0:T(8,128)}, u32[]{:S(2)}, u32[]{:S(2)}) collective-permute-start(f32[1,2,2,256,256]{3,4,1,2,0:T(8,128)S(1)} %broadcast_select_fusion.6), channel_id=1, source_target_pairs={{0,16},{8,24},{16,0},{24,8},{1,17},{9,25},{17,1},{25,9},{2,18},{10... | collective-permute-start | bytes 3145736 | tf_op jit(solution)/shard_map/ppermute | solution.py:20
  288.0 1.7 copy-start.1
  290.3 1.4 copy-start
Sparse Core Ops, SparseCore 0:
  138.1 149.8 all-reduce.2
where the time goes:
time: 312 us
  waiting for transfers between devices  222 us (71%)
  starting transfers between devices  35.7 us (11%)
  between operations  24.2 us (8%)
  matrix products  14.1 us (5%)
  other arithmetic  10.9 us (3%)
  local copies, waits for them, and re-layouts  4.38 us (1%)
    psum x1, waiting for transfers between devices, spread(): return lax.psum(jnp.where(mine, array, jnp.zeros_like(array)), axis)  142 us
    ppermute x5, waiting for transfers between devices, passed_along(): return lax.ppermute(block, axis, route)  62.2 us
    ppermute x5, starting transfers between devices, passed_along(): return lax.ppermute(block, axis, route)  32.3 us
    ppermute x4, waiting for transfers between devices, shifted(): lax.ppermute(array, axis, [(i, (i + by) % devices) for i in range(devices)])  18 us
    dot_general x8, matrix products, matmul_right(): jnp.einsum('...ij,kj->...ik', left, right, precision=lax.Precision.HIGHEST)  8.18 us
  transfers between devices with their start and end apart: 10, of which 7 were waited for; matrix products, arithmetic and copies ran while one was open for 4% of the time, Pallas kernels for 0%

commit v1 on v0

--- a/solution.py
+++ b/solution.py
@@ -6,7 +6,7 @@
 
 def spread(array, axis, root):
     mine = lax.axis_index(axis) == root
-    return lax.psum(jnp.where(mine, array, jnp.zeros_like(array)), axis)
+    return jnp.sum(lax.all_gather(jnp.where(mine, array, jnp.zeros_like(array)), axis), axis=0)
 
 
 def passed_along(block, axis, distance):

time: 312 us -> 374 us (1.20)
  the two profiles are of different devices: /device:TPU:0 before, /device:TPU:5 now
where the time goes in v1:
time: 374 us; the launch traced here: 373 us
  waiting for transfers between devices  266 us (71%)
  starting transfers between devices  39.3 us (11%)
  other arithmetic  24.9 us (7%)
  between operations  24.2 us (6%)
  matrix products  15 us (4%)
  local copies, waits for them, and re-layouts  3.92 us (1%)
    ppermute x5, waiting for transfers between devices, passed_along(): return lax.ppermute(block, axis, route)  155 us
    ppermute x4, waiting for transfers between devices, shifted(): lax.ppermute(array, axis, [(i, (i + by) % devices) for i in range(devices)])  82 us
    ppermute x5, starting transfers between devices, passed_along(): return lax.ppermute(block, axis, route)  31.3 us
    all_gather x2, waiting for transfers between devices, spread(): lax.all_gather(jnp.where(mine, array, jnp.zeros_like(array)), axis)  28.3 us
    reduce_sum x2, other arithmetic, spread(): jnp.sum(lax.all_gather(jnp.where(mine, array, jnp.zeros_like(array)), axi...  13.9 us
    dot_general x8, matrix products, matmul_right(): jnp.einsum('...ij,kj->...ik', left, right, precision=lax.Precision.HIGHEST)  8.41 us
    ppermute x4, starting transfers between devices, shifted(): lax.ppermute(array, axis, [(i, (i + by) % devices) for i in range(devices)])  7.97 us
  transfers between devices with their start and end apart: 11, of which 9 were waited for; matrix products, arithmetic and copies ran while one was open for 5% of the time, Pallas kernels for 0%

profile of v1, /device:TPU:5, one launch (start us, length us, event | category | flops | bytes accessed | tf_op | source)
XLA Modules:
  0.0 373.4 jit_solution(8919216343084254180)
XLA Ops:
  6.5 1.3 fusion.18
  9.2 2.1 broadcast_select_fusion.8
  12.5 3.1 collective-permute-start
  20.1 28.5 %collective-permute-done = f32[1,2,2,256,256]{3,4,1,2,0:T(8,128)} collective-permute-done((f32[1,2,2,256,256]{3,4,1,2,0:T(8,128)S(1)}, f32[1,2,2,256,256]{3,4,1,2,0:T(8,128)}, u32[]{:S(2)}, u32[]{:S(2)}) %collective-permute-start) | collective-permute-done | bytes 1048608 | tf_op jit(solution)/shard_map/ppermute | solution.py:15
  48.9 5.1 %collective-permute-start.5 = (f32[1,2,2,256,256]{3,4,1,2,0:T(8,128)S(1)}, f32[1,2,2,256,256]{3,4,1,2,0:T(8,128)}, u32[]{:S(2)}, u32[]{:S(2)}) collective-permute-start(f32[1,2,2,256,256]{3,4,1,2,0:T(8,128)S(1)} %get-tuple-element.5), channel_id=1, source_target_pairs={{0,1},{1,2},{2,3},{3,4},{4,5},{5,6},{6,7},{8,9},{9,10},{10,11},{11... | collective-permute-start | bytes 3145736 | tf_op jit(solution)/shard_map/ppermute | solution.py:15
  54.0 1.9 collective-permute-start.1
  57.3 38.3 %collective-permute-done.5 = f32[1,2,2,256,256]{3,4,1,2,0:T(8,128)} collective-permute-done((f32[1,2,2,256,256]{3,4,1,2,0:T(8,128)S(1)}, f32[1,2,2,256,256]{3,4,1,2,0:T(8,128)}, u32[]{:S(2)}, u32[]{:S(2)}) %collective-permute-start.5) | collective-permute-done | bytes 1048608 | tf_op jit(solution)/shard_map/ppermute | solution.py:15
  95.8 4.3 %collective-permute-start.6 = (f32[1,2,2,256,256]{3,4,1,2,0:T(8,128)S(1)}, f32[1,2,2,256,256]{3,4,1,2,0:T(8,128)}, u32[]{:S(2)}, u32[]{:S(2)}) collective-permute-start(f32[1,2,2,256,256]{3,4,1,2,0:T(8,128)S(1)} %broadcast_select_fusion), channel_id=1, source_target_pairs={{0,2},{1,3},{2,4},{3,5},{4,6},{5,7},{8,10},{9,11},{10,12},{11,13},... | collective-permute-start | bytes 3145736 | tf_op jit(solution)/shard_map/ppermute | solution.py:15
  100.1 37.4 %collective-permute-done.1 = f32[1,2,2,256,256]{3,4,1,2,0:T(8,128)} collective-permute-done((f32[1,2,2,256,256]{3,4,1,2,0:T(8,128)S(1)}, f32[1,2,2,256,256]{3,4,1,2,0:T(8,128)}, u32[]{:S(2)}, u32[]{:S(2)}) %collective-permute-start.1) | collective-permute-done | bytes 1048608 | tf_op jit(solution)/shard_map/ppermute | solution.py:15
  137.5 1.4 broadcast_select_fusion.4
  138.9 16.8 %collective-permute-start.2 = (f32[1,2,2,256,256]{3,4,1,2,0:T(8,128)S(1)}, f32[1,2,2,256,256]{3,4,1,2,0:T(8,128)}, u32[]{:S(2)}, u32[]{:S(2)}) collective-permute-start(f32[1,2,2,256,256]{3,4,1,2,0:T(8,128)S(1)} %broadcast_select_fusion.4), channel_id=1, source_target_pairs={{0,2},{1,3},{2,4},{3,5},{4,6},{5,7},{8,10},{9,11},{10,12},{11,13},... | collective-permute-start | bytes 3145736 | tf_op jit(solution)/shard_map/ppermute | solution.py:15
  155.6 26.8 %collective-permute-done.6 = f32[1,2,2,256,256]{3,4,1,2,0:T(8,128)} collective-permute-done((f32[1,2,2,256,256]{3,4,1,2,0:T(8,128)S(1)}, f32[1,2,2,256,256]{3,4,1,2,0:T(8,128)}, u32[]{:S(2)}, u32[]{:S(2)}) %collective-permute-start.6) | collective-permute-done | bytes 1048608 | tf_op jit(solution)/shard_map/ppermute | solution.py:15
  182.4 1.4 broadcast_select_fusion.1
  183.8 4.0 %collective-permute-start.7 = (f32[1,2,2,256,256]{3,4,1,2,0:T(8,128)S(1)}, f32[1,2,2,256,256]{3,4,1,2,0:T(8,128)}, u32[]{:S(2)}, u32[]{:S(2)}) collective-permute-start(f32[1,2,2,256,256]{3,4,1,2,0:T(8,128)S(1)} %broadcast_select_fusion.1), channel_id=1, source_target_pairs={{0,8},{8,16},{16,24},{24,0},{1,9},{9,17},{17,25},{25,1},{2,10},{10... | collective-permute-start | bytes 3145736 | tf_op jit(solution)/shard_map/ppermute | solution.py:20
  187.8 24.0 %collective-permute-done.2 = f32[1,2,2,256,256]{3,4,1,2,0:T(8,128)} collective-permute-done((f32[1,2,2,256,256]{3,4,1,2,0:T(8,128)S(1)}, f32[1,2,2,256,256]{3,4,1,2,0:T(8,128)}, u32[]{:S(2)}, u32[]{:S(2)}) %collective-permute-start.2) | collective-permute-done | bytes 1048608 | tf_op jit(solution)/shard_map/ppermute | solution.py:15
  211.8 1.4 broadcast_select_fusion.5
  213.2 3.6 collective-permute-start.3
  221.2 1.4 broadcast_select_fusion.2
  223.0 15.5 %collective-permute-done.3 = f32[1,2,2,256,256]{3,4,1,2,0:T(8,128)} collective-permute-done((f32[1,2,2,256,256]{3,4,1,2,0:T(8,128)S(1)}, f32[1,2,2,256,256]{3,4,1,2,0:T(8,128)}, u32[]{:S(2)}, u32[]{:S(2)}) %collective-permute-start.3) | collective-permute-done | bytes 1048608 | tf_op jit(solution)/shard_map/ppermute | solution.py:20
  238.8 32.9 %collective-permute-done.8 = f32[1,2,2,256,256]{3,4,1,2,0:T(8,128)} collective-permute-done((f32[1,2,2,256,256]{3,4,1,2,0:T(8,128)S(1)}, f32[1,2,2,256,256]{3,4,1,2,0:T(8,128)}, u32[]{:S(2)}, u32[]{:S(2)}) %collective-permute-start.8) | collective-permute-done | bytes 1048608 | tf_op jit(solution)/shard_map/ppermute | solution.py:20
  271.7 1.4 broadcast_select_fusion.3
  273.0 33.6 %collective-permute-done.4 = f32[1,2,2,256,256]{3,4,1,2,0:T(8,128)} collective-permute-done((f32[1,2,2,256,256]{3,4,1,2,0:T(8,128)S(1)}, f32[1,2,2,256,256]{3,4,1,2,0:T(8,128)}, u32[]{:S(2)}, u32[]{:S(2)}) %collective-permute-start.4) | collective-permute-done | bytes 1048608 | tf_op jit(solution)/shard_map/ppermute | solution.py:20
  306.7 1.4 broadcast_select_fusion.7
  308.1 7.0 %reduce_sum.19 = f32[2,256,256]{2,1,0:T(8,128)S(1)} reduce(f32[32,1,2,256,256]{4,3,2,1,0:T(8,128)} %all-gather.7.cloned.1.call-done, f32[]{:T(128)} %constant.155.clone.1), dimensions={0,1}, to_apply=%region_1.2 | reduce | flops 4063232 | bytes 17301508 | tf_op jit(solution)/shard_map/reduce_sum | solution.py:9
  315.1 1.4 fusion.12
  316.5 1.4 fusion.13
  317.9 28.3 %all-gather.5.cloned.1.call-done = f32[32,1,2,256,256]{4,3,2,1,0:T(8,128)} async-done(((f32[1,1,2,256,256]{4,3,2,1,0:T(8,128)}), f32[32,1,2,256,256]{4,3,2,1,0:T(8,128)}) %all-gather.5.cloned.1.call-update) | async-done | bytes 16777232 | tf_op jit(solution)/shard_map/all_gather | solution.py:9
  346.2 6.9 %reduce_sum.18 = f32[2,256,256]{2,1,0:T(8,128)S(1)} reduce(f32[32,1,2,256,256]{4,3,2,1,0:T(8,128)} %all-gather.5.cloned.1.call-done, f32[]{:T(128)} %constant.155.clone.1), dimensions={0,1}, to_apply=%region_0.1 | reduce | flops 4063232 | bytes 17301508 | tf_op jit(solution)/shard_map/reduce_sum | solution.py:9
  357.7 1.0 fusion
  360.4 1.2 fusion.14
  363.3 1.0 fusion.4
  365.5 1.0 copy.27
  (42 shorter events, 12.2 us)
Async XLA Ops:
  6.5 5.6 %copy-start.5 = (f32[1,2,2,256,256]{4,3,2,1,0:T(8,128)S(1)}, f32[1,2,2,256,256]{4,3,2,1,0:T(8,128)}, u32[]{:S(2)}) copy-start(f32[1,2,2,256,256]{4,3,2,1,0:T(8,128)} %param.5) | copy-start | bytes 3145732
  6.5 301.5 %all-gather.7.cloned.1.call-start = ((), (), s32[]{:S(2)}) async-start(), calls=%async_computation.1 | async-start | bytes 17301504 | tf_op jit(solution)/shard_map/all_gather | solution.py:9
  9.2 6.4 %copy-start.6 = (s32[2]{0:T(128)S(1)}, s32[2]{0:T(128)}, u32[]{:S(2)}) copy-start(s32[2]{0:T(128)} %param.9) | copy-start | bytes 28
  11.3 334.8 %all-gather.5.cloned.1.call-start = ((), (), s32[]{:S(2)}) async-start(), calls=%async_computation | async-start | bytes 17301504 | tf_op jit(solution)/shard_map/all_gather | solution.py:9
  12.5 36.2 %collective-permute-start = (f32[1,2,2,256,256]{3,4,1,2,0:T(8,128)S(1)}, f32[1,2,2,256,256]{3,4,1,2,0:T(8,128)}, u32[]{:S(2)}, u32[]{:S(2)}) collective-permute-start(f32[1,2,2,256,256]{3,4,1,2,0:T(8,128)S(1)} %copy.17), channel_id=1, source_target_pairs={{0,1},{1,2},{2,3},{3,4},{4,5},{5,6},{6,7},{8,9},{9,10},{10,11},{11... | collective-permute-start | bytes 3145736 | tf_op jit(solution)/shard_map/ppermute | solution.py:15
  48.9 46.7 %collective-permute-start.5 = (f32[1,2,2,256,256]{3,4,1,2,0:T(8,128)S(1)}, f32[1,2,2,256,256]{3,4,1,2,0:T(8,128)}, u32[]{:S(2)}, u32[]{:S(2)}) collective-permute-start(f32[1,2,2,256,256]{3,4,1,2,0:T(8,128)S(1)} %get-tuple-element.5), channel_id=1, source_target_pairs={{0,1},{1,2},{2,3},{3,4},{4,5},{5,6},{6,7},{8,9},{9,10},{10,11},{11... | collective-permute-start | bytes 3145736 | tf_op jit(solution)/shard_map/ppermute | solution.py:15
  54.0 83.5 %collective-permute-start.1 = (f32[1,2,2,256,256]{3,4,1,2,0:T(8,128)S(1)}, f32[1,2,2,256,256]{3,4,1,2,0:T(8,128)}, u32[]{:S(2)}, u32[]{:S(2)}) collective-permute-start(f32[1,2,2,256,256]{3,4,1,2,0:T(8,128)S(1)} %get-tuple-element.6), channel_id=1, source_target_pairs={{0,1},{1,2},{2,3},{3,4},{4,5},{5,6},{6,7},{8,9},{9,10},{10,11},{11... | collective-permute-start | bytes 3145736 | tf_op jit(solution)/shard_map/ppermute | solution.py:15
  95.8 86.7 %collective-permute-start.6 = (f32[1,2,2,256,256]{3,4,1,2,0:T(8,128)S(1)}, f32[1,2,2,256,256]{3,4,1,2,0:T(8,128)}, u32[]{:S(2)}, u32[]{:S(2)}) collective-permute-start(f32[1,2,2,256,256]{3,4,1,2,0:T(8,128)S(1)} %broadcast_select_fusion), channel_id=1, source_target_pairs={{0,2},{1,3},{2,4},{3,5},{4,6},{5,7},{8,10},{9,11},{10,12},{11,13},... | collective-permute-start | bytes 3145736 | tf_op jit(solution)/shard_map/ppermute | solution.py:15
  138.9 48.9 %copy-start.1 = (f32[1,2,2,256,256]{3,4,1,2,0:T(8,128)}, f32[1,2,2,256,256]{3,4,1,2,0:T(8,128)S(1)}, u32[]{:S(2)}) copy-start(f32[1,2,2,256,256]{3,4,1,2,0:T(8,128)S(1)} %broadcast_select_fusion.4) | copy-start | bytes 3145732
  138.9 72.9 %collective-permute-start.2 = (f32[1,2,2,256,256]{3,4,1,2,0:T(8,128)S(1)}, f32[1,2,2,256,256]{3,4,1,2,0:T(8,128)}, u32[]{:S(2)}, u32[]{:S(2)}) collective-permute-start(f32[1,2,2,256,256]{3,4,1,2,0:T(8,128)S(1)} %broadcast_select_fusion.4), channel_id=1, source_target_pairs={{0,2},{1,3},{2,4},{3,5},{4,6},{5,7},{8,10},{9,11},{10,12},{11,13},... | collective-permute-start | bytes 3145736 | tf_op jit(solution)/shard_map/ppermute | solution.py:15
  183.8 32.9 %copy-start.7 = (s32[2]{0:T(128)S(1)}, s32[2]{0:T(128)}, u32[]{:S(2)}) copy-start(s32[2]{0:T(128)} %param.8) | copy-start | bytes 28
  183.8 37.4 %collective-permute-start.7 = (f32[1,2,2,256,256]{3,4,1,2,0:T(8,128)S(1)}, f32[1,2,2,256,256]{3,4,1,2,0:T(8,128)}, u32[]{:S(2)}, u32[]{:S(2)}) collective-permute-start(f32[1,2,2,256,256]{3,4,1,2,0:T(8,128)S(1)} %broadcast_select_fusion.1), channel_id=1, source_target_pairs={{0,8},{8,16},{16,24},{24,0},{1,9},{9,17},{17,25},{25,1},{2,10},{10... | collective-permute-start | bytes 3145736 | tf_op jit(solution)/shard_map/ppermute | solution.py:20
  213.2 25.3 %collective-permute-start.3 = (f32[1,2,2,256,256]{3,4,1,2,0:T(8,128)S(1)}, f32[1,2,2,256,256]{3,4,1,2,0:T(8,128)}, u32[]{:S(2)}, u32[]{:S(2)}) collective-permute-start(f32[1,2,2,256,256]{3,4,1,2,0:T(8,128)S(1)} %broadcast_select_fusion.5), channel_id=1, source_target_pairs={{0,8},{8,16},{16,24},{24,0},{1,9},{9,17},{17,25},{25,1},{2,10},{10... | collective-permute-start | bytes 3145736 | tf_op jit(solution)/shard_map/ppermute | solution.py:20
  222.6 16.1 %copy-start = (f32[1,2,2,256,256]{3,4,1,2,0:T(8,128)}, f32[1,2,2,256,256]{3,4,1,2,0:T(8,128)S(1)}, u32[]{:S(2)}) copy-start(f32[1,2,2,256,256]{3,4,1,2,0:T(8,128)S(1)} %broadcast_select_fusion.2) | copy-start | bytes 3145732
  222.6 49.0 %collective-permute-start.8 = (f32[1,2,2,256,256]{3,4,1,2,0:T(8,128)S(1)}, f32[1,2,2,256,256]{3,4,1,2,0:T(8,128)}, u32[]{:S(2)}, u32[]{:S(2)}) collective-permute-start(f32[1,2,2,256,256]{3,4,1,2,0:T(8,128)S(1)} %broadcast_select_fusion.2), channel_id=1, source_target_pairs={{0,16},{8,24},{16,0},{24,8},{1,17},{9,25},{17,1},{25,9},{2,18},{10... | collective-permute-start | bytes 3145736 | tf_op jit(solution)/shard_map/ppermute | solution.py:20
  238.6 34.4 %copy-start.2 = (f32[1,2,2,256,256]{3,4,1,2,0:T(8,128)}, f32[1,2,2,256,256]{3,4,1,2,0:T(8,128)S(1)}, u32[]{:S(2)}) copy-start(f32[1,2,2,256,256]{3,4,1,2,0:T(8,128)S(1)} %broadcast_select_fusion.6) | copy-start | bytes 3145732
  238.6 68.1 %collective-permute-start.4 = (f32[1,2,2,256,256]{3,4,1,2,0:T(8,128)S(1)}, f32[1,2,2,256,256]{3,4,1,2,0:T(8,128)}, u32[]{:S(2)}, u32[]{:S(2)}) collective-permute-start(f32[1,2,2,256,256]{3,4,1,2,0:T(8,128)S(1)} %broadcast_select_fusion.6), channel_id=1, source_target_pairs={{0,16},{8,24},{16,0},{24,8},{1,17},{9,25},{17,1},{25,9},{2,18},{10... | collective-permute-start | bytes 3145736 | tf_op jit(solution)/shard_map/ppermute | solution.py:20
  353.1 1.3 copy-start.4
  353.7 2.3 copy-start.3
Sparse Core Ops, SparseCore 0:
  11.5 177.2 all-gather.6
  191.9 154.2 all-gather.4
